TPU v7x, 32 devices: a whole 2x2x4 slice. The times are simulated.
32 devices in a mesh: groups: 2 (over y), img: 4 (over z), ref: 2 (over x), rep: 2 (over core).
Axes of the slice: x: 2, y: 2, z: 4, core: 2. Of those that a mesh axis runs over, the one named last changes fastest.
Arguments:
- images: float32 [768, 4096], P(('groups', 'img')), parts along dimension 0, may hold values from -24 to 24
- references: float32 [4096, 2048], P('img', ('groups', 'ref', 'rep')), parts along dimension 1, may hold values from -1.2 to 1.2
- rotations: int32 [2048], P(('groups', 'ref', 'rep')), parts along dimension 0, may hold values from 0 to 7
- image_group: int32 [768], P(('groups', 'img')), parts along dimension 0, may hold values from 0 to 15
- noise_var: float32 [16], replicated, may hold values from 0.5 to 2
Outputs:
- class_means: float32 [4096, 2048], P('img', ('groups', 'ref', 'rep')), parts along dimension 1
- class_weights: float32 [2048], P(('groups', 'ref', 'rep')), parts along dimension 0
- log_evidence: float32 [768], P(('groups', 'img')), parts along dimension 0
There are 2 independent parts, one for each index of `groups`. A program takes and returns all parts, laid end to end along the dimension named above; an argument that names none is the same for every part. Nothing has to cross between parts.
All inputs are finite; a program needn't handle non-finite values.
Results may differ from a plain program's by a relative error of at most 0.0003.
Values sent between devices are 32-bit elements; how exact they have to be, the bound alone decides.
A program may use at most 64 MiB of HBM per device.

v0:
```python
import jax
import jax.numpy as jnp
from jax import lax
from jax.sharding import PartitionSpec as P

IMAGE_SIDE = 64
PIXELS = 4096


def joined(part, axis, combine):
    gathered = jax.tree.map(lambda a: lax.all_gather(a, axis), part)

    def take(source):
        return jax.tree.map(lambda a: lax.dynamic_index_in_dim(a, source, 0, False), gathered)

    return lax.fori_loop(
        1, lax.axis_size(axis), lambda source, state: combine(state, take(source)), take(0)
    )


def turn_forward(field, which):
    quarter = which % 4
    base = field if which < 4 else jnp.swapaxes(field, 0, 1)
    return jnp.rot90(base, quarter, axes=(0, 1))


def turn_inverse(field, which):
    quarter = which % 4
    base = jnp.rot90(field, -quarter, axes=(0, 1))
    return base if which < 4 else jnp.swapaxes(base, 0, 1)


def select_turn(field, rotations, turner):
    result = jnp.zeros_like(field)
    for which in range(8):
        result = jnp.where(rotations[None, None, :] == which, turner(field, which), result)
    return result


def combine_stats(first, second):
    top = jnp.maximum(first[0], second[0])
    total = first[1] * jnp.exp(first[0] - top) + second[1] * jnp.exp(second[0] - top)
    return (top, total)


def body(images, references, rotations, image_group, noise_var):
    gathered = lax.all_gather(references, "img", axis=0, tiled=True)
    rotated = select_turn(
        gathered.reshape(IMAGE_SIDE, IMAGE_SIDE, -1), rotations, turn_inverse
    ).reshape(PIXELS, -1)
    norms = jnp.sum(gathered * gathered, axis=0)
    group_hot = image_group[:, None] == jnp.arange(noise_var.shape[0])[None, :]
    sigma = jnp.sum(jnp.where(group_hot, noise_var[None, :], 0.0), axis=1)
    scores = (
        jnp.dot(
            images, rotated, precision=lax.Precision.HIGHEST, preferred_element_type=jnp.float32
        )
        - 0.5 * norms[None, :]
    ) / sigma[:, None]
    local_top = jnp.max(scores, axis=1)
    local_total = jnp.sum(jnp.exp(scores - local_top[:, None]), axis=1)
    top, total = joined((local_top, local_total), ("ref", "rep"), combine_stats)
    log_evidence = top + jnp.log(total)
    posterior = jnp.exp(scores - log_evidence[:, None])
    weight_sum = lax.psum(jnp.sum(posterior, axis=0), "img")
    numer_image = lax.dot_general(
        images,
        posterior,
        (((0,), (0,)), ((), ())),
        precision=lax.Precision.HIGHEST,
        preferred_element_type=jnp.float32,
    )
    numerator = select_turn(
        numer_image.reshape(IMAGE_SIDE, IMAGE_SIDE, -1), rotations, turn_forward
    ).reshape(PIXELS, -1)
    owned = lax.psum_scatter(numerator, "img", scatter_dimension=0, tiled=True)
    class_means = owned / (weight_sum + 1.0)[None, :]
    class_total = weight_sum.shape[0] * lax.axis_size("ref") * lax.axis_size("rep")
    image_total = images.shape[0] * lax.axis_size("img")
    class_weights = weight_sum * (class_total / image_total)
    return (class_means, class_weights, log_evidence)


def solution(mesh):
    placed = (
        P(("groups", "img"), None),
        P("img", ("groups", "ref", "rep")),
        P(("groups", "ref", "rep")),
        P(("groups", "img")),
        P(),
    )
    return jax.shard_map(
        body,
        mesh=mesh,
        in_specs=placed,
        out_specs=(
            P("img", ("groups", "ref", "rep")),
            P(("groups", "ref", "rep")),
            P(("groups", "img")),
        ),
        check_vma=False,
    )
```

profile of v0, /device:TPU:0, one launch (start us, length us, event | category | flops | bytes accessed | tf_op | source)
XLA Modules:
  0.0 286.7 jit_solution(2013551750306974672)
XLA Ops:
  7.2 0.0 copy-start
  7.2 0.0 all-gather.4.cloned.1.call-start
  7.2 0.7 all-gather.4.cloned.1.call-update
  7.9 0.0 reduce-scatter.2.cloned.1.call-start
  8.0 1.2 dynamic-slice
  9.9 0.8 select_reduce_fusion
  10.6 0.7 broadcast_compare_fusion.7
  11.3 81.7 %all-gather.4.cloned.1.call-done = f32[4096,256]{1,0:T(8,128)} async-done(((f32[1024,256]{1,0:T(8,128)}), f32[4096,256]{1,0:T(8,128)}) %all-gather.4.cloned.1.call-update) | async-done | bytes 4194320 | tf_op jit(solution)/shard_map/all_gather | solution.py:47
  93.1 6.6 %rev.41 = f32[64,64,256]{2,1,0:T(8,128)} reverse(f32[64,64,256]{2,1,0:T(8,128)} %bitcast.41), dimensions={0,1} | reverse | bytes 8388608 | tf_op jit(solution)/shard_map/jit(rot90)/jit(_flip)/rev | solution.py:29
  99.7 6.7 %rev.40 = f32[64,64,256]{2,1,0:T(8,128)} reverse(f32[64,64,256]{2,1,0:T(8,128)} %bitcast.42), dimensions={1} | reverse | bytes 8388608 | tf_op jit(solution)/shard_map/jit(rot90)/jit(_flip)/rev | solution.py:29
  106.4 4.7 %rev.42 = f32[64,64,256]{2,0,1:T(8,128)} reverse(f32[64,64,256]{2,0,1:T(8,128)} %bitcast.43), dimensions={1} | reverse | bytes 8388608 | tf_op jit(solution)/shard_map/jit(rot90)/jit(_flip)/rev | solution.py:29
  111.0 0.0 copy-start.1
  111.0 2.9 %multiply_reduce_fusion = f32[256]{0:T(256)S(1)} fusion(f32[4096,256]{1,0:T(8,128)} %all-gather.4.cloned.1.call-done), kind=kLoop, calls=%fused_computation.22 | loop fusion | flops 2096896 | bytes 4195328 | tf_op jit(solution)/shard_map/reduce_sum | solution.py:51
  113.9 0.5 copy-done.1
  114.5 16.2 %fusion.3 = f32[64,64,256]{2,1,0:T(8,128)S(1)} fusion(f32[64,64,256]{2,1,0:T(8,128)} %rev.40, f32[64,64,256]{2,0,1:T(8,128)} %rev.42, f32[64,64,256]{2,0,1:T(8,128)} %bitcast.52, f32[64,64,256]{2,0,1:T(8,128)S(1)} %bitcast.45, f32[64,64,256]{2,0,1:T(8,128)} %bitcast.53, f32[64,64,256]{2,1,0:T(8,128)} %rev.41, f32[64,64,256]{2,1,0:T(8,128)S(1)} %bitcast.44, ...), kind=kLoop, calls=%fused_computation.9 | loop fusion | flops 8388608 | bytes 33556480 | tf_op jit(solution)/shard_map/jit(_where)/select_n | solution.py:36
  130.7 0.0 copy-done
  130.7 2.6 fusion.13
  133.3 0.2 exponential_reduce_fusion
  133.5 0.2 dynamic-update-slice
  133.7 0.2 dynamic-update-slice.1
  133.9 6.6 %all-reduce.2 = (f32[384]{0:T(512)S(1)}, f32[384]{0:T(512)S(1)}) all-reduce(f32[384]{0:T(512)S(1)} %dynamic-update-slice, f32[384]{0:T(512)S(1)} %dynamic-update-slice.1), channel_id=2, replica_groups=mesh['groups'=2,'img'=4,'ref'=2,'rep'=2] {'ref','rep'}, use_global_device_ids=true, to_apply=%add | all-reduce | flops 768 | bytes 6144
  140.5 0.1 reshape.48
  140.6 0.1 reshape.49
  140.7 0.1 while.17
  140.8 0.0 copy-start.2
  140.8 5.3 %convolution_bitcast_fusion = f32[4096,256]{0,1:T(8,128)} fusion(f32[96,4096]{1,0:T(8,128)S(1)} %copy-done, f32[256,96]{0,1:T(8,128)S(1)} %get-tuple-element.163, f32[96]{0:T(128)S(1)} %log_add_fusion), kind=kOutput, calls=%fused_computation.6 | convolution fusion | flops 1207984128 | bytes 5865856 | tf_op jit(solution)/shard_map/dot_general | solution.py:66
  146.1 5.6 %copy.31 = f32[4096,256]{1,0:T(8,128)} copy(f32[4096,256]{0,1:T(8,128)} %convolution_bitcast_fusion) | data formatting | bytes 8388608 | tf_op jit(solution)/shard_map/dot_general | solution.py:66
  151.7 6.6 %copy.64 = f32[64,64,256]{2,0,1:T(8,128)} copy(f32[64,64,256]{2,1,0:T(8,128)} %bitcast.46) | data formatting | bytes 8388608 | tf_op jit(solution)/shard_map/reshape | solution.py:74
  158.2 6.7 %rev.45 = f32[64,64,256]{2,1,0:T(8,128)} reverse(f32[64,64,256]{2,1,0:T(8,128)} %bitcast.54), dimensions={1} | reverse | bytes 8388608 | tf_op jit(solution)/shard_map/jit(rot90)/jit(_flip)/rev | solution.py:24
  164.9 6.7 %rev.44 = f32[64,64,256]{2,1,0:T(8,128)} reverse(f32[64,64,256]{2,1,0:T(8,128)} %bitcast.55), dimensions={0,1} | reverse | bytes 8388608 | tf_op jit(solution)/shard_map/jit(rot90)/jit(_flip)/rev | solution.py:24
  171.6 6.6 %rev.43 = f32[64,64,256]{2,1,0:T(8,128)} reverse(f32[64,64,256]{2,1,0:T(8,128)} %bitcast.47), dimensions={1} | reverse | bytes 8388608 | tf_op jit(solution)/shard_map/jit(rot90)/jit(_flip)/rev | solution.py:24
  178.2 6.6 %rev.46 = f32[64,64,256]{2,1,0:T(8,128)} reverse(f32[64,64,256]{2,1,0:T(8,128)} %bitcast.48), dimensions={0,1} | reverse | bytes 8388608 | tf_op jit(solution)/shard_map/jit(rot90)/jit(_flip)/rev | solution.py:24
  184.9 17.6 %fusion.5 = f32[64,64,256]{2,1,0:T(8,128)} fusion(f32[64,64,256]{2,1,0:T(8,128)} %rev.43, f32[64,64,256]{2,1,0:T(8,128)} %rev.44, f32[64,64,256]{2,0,1:T(8,128)} %bitcast.50, f32[64,64,256]{2,1,0:T(8,128)} %rev.45, f32[64,64,256]{2,1,0:T(8,128)} %rev.46, f32[64,64,256]{2,0,1:T(8,128)} %bitcast.51, f32[64,64,256]{2,1,0:T(8,128)} %bitcast.49, ...), kind=kLoop, calls=%fused_computation.12 | loop fusion | flops 8388608 | bytes 33556480 | tf_op jit(solution)/shard_map/jit(_where)/select_n | solution.py:36
  202.5 0.0 reduce-scatter.2.cloned.1.call-update
  202.5 0.0 copy-done.2
  202.5 0.1 fusion.11
  202.6 9.8 %psum.7 = f32[256]{0:T(256)S(1)} all-reduce(f32[256]{0:T(256)S(1)} %fusion.11), channel_id=1, replica_groups=mesh['groups'=2,'img'=4,'ref'=2,'rep'=2] {'img'}, use_global_device_ids=true, to_apply=%region_8.9 | all-reduce | flops 256 | bytes 2048 | tf_op jit(solution)/shard_map/psum | solution.py:65
  212.4 0.6 broadcast_multiply_fusion
  212.9 64.6 %reduce-scatter.2.cloned.1.call-done = f32[1024,256]{1,0:T(8,128)} async-done(((f32[4096,256]{1,0:T(8,128)}), f32[1024,256]{1,0:T(8,128)}) %reduce-scatter.2.cloned.1.call-update) | async-done | bytes 1048592 | tf_op jit(solution)/shard_map/reduce_scatter | solution.py:76
  277.6 2.3 broadcast_divide_fusion
  (9 shorter events, 0.1 us)
Async XLA Ops:
  7.2 123.5 %copy-start = (f32[96,4096]{1,0:T(8,128)S(1)}, f32[96,4096]{1,0:T(8,128)}, u32[]{:S(2)}) copy-start(f32[96,4096]{1,0:T(8,128)} %param.7) | copy-start | bytes 4718596
  7.2 85.9 %all-gather.4.cloned.1.call-start = ((), (), s32[]{:S(2)}) async-start(), calls=%async_computation.1 | async-start | bytes 5242880 | tf_op jit(solution)/shard_map/all_gather | solution.py:47
  7.9 269.6 %reduce-scatter.2.cloned.1.call-start = ((), (), s32[]{:S(2)}) async-start(), calls=%async_computation.2 | async-start | bytes 5242880 | tf_op jit(solution)/shard_map/reduce_scatter | solution.py:76
  111.0 3.4 %copy-start.1 = (f32[4096,256]{1,0:T(8,128)S(1)}, f32[4096,256]{1,0:T(8,128)}, u32[]{:S(2)}) copy-start(f32[4096,256]{1,0:T(8,128)} %all-gather.4.cloned.1.call-done) | copy-start | bytes 12582916
  140.8 61.7 %copy-start.2 = (f32[96]{0:T(128)}, f32[96]{0:T(128)S(1)}, u32[]{:S(2)}) copy-start(f32[96]{0:T(128)S(1)} %log_add_fusion) | copy-start | bytes 1156
Sparse Core Ops, SparseCore 0:
  9.6 83.4 all-gather.3
  202.6 74.9 reduce-scatter.1
where the time goes:
time: 288 us; the launch traced here: 287 us
  waiting for transfers between devices  147 us (51%)
  local copies, waits for them, and re-layouts  59.2 us (21%)
  other arithmetic  41.3 us (14%)
  blocking collectives  16.3 us (6%)
  between operations  14.8 us (5%)
  matrix products  7.87 us (3%)
    all_gather x1, waiting for transfers between devices, body(): gathered = lax.all_gather(references, 'img', axis=0, tiled=True)  81.7 us
    reduce_scatter x1, waiting for transfers between devices, body(): owned = lax.psum_scatter(numerator, 'img', scatter_dimension=0, tiled=True)  64.6 us
    select_n x2, other arithmetic, select_turn(): jnp.where(rotations[None, None, :] == which, turner(field, which), result)  33.8 us
    rev x4, local copies, waits for them, and re-layouts, turn_forward(): return jnp.rot90(base, quarter, axes=(0, 1))  26.6 us
    rev x3, local copies, waits for them, and re-layouts, turn_inverse(): base = jnp.rot90(field, -quarter, axes=(0, 1))  18 us
    psum x1, blocking collectives, body(): weight_sum = lax.psum(jnp.sum(posterior, axis=0), 'img')  9.77 us
    reshape x1, local copies, waits for them, and re-layouts, body(): numer_image.reshape(IMAGE_SIDE, IMAGE_SIDE, -1)  6.57 us
    unnamed x1, blocking collectives  6.57 us
  transfers between devices with their start and end apart: 2, of which 2 were waited for; matrix products, arithmetic and copies ran while one was open for 1% of the time, Pallas kernels for 0%

commit v1 on v0

--- a/solution.py
+++ b/solution.py
@@ -44,7 +44,15 @@
 
 
 def body(images, references, rotations, image_group, noise_var):
-    gathered = lax.all_gather(references, "img", axis=0, tiled=True)
+    gathered = jnp.concatenate(
+        jax.lax.all_to_all(
+            jnp.stack([references] * jax.lax.axis_size("img"), 0),
+            "img",
+            split_axis=0,
+            concat_axis=0,
+        ),
+        0,
+    )
     rotated = select_turn(
         gathered.reshape(IMAGE_SIDE, IMAGE_SIDE, -1), rotations, turn_inverse
     ).reshape(PIXELS, -1)

time: 288 us -> 314 us (1.090)
  waiting for transfers between devices: 147 us -> 158 us
  local copies, waits for them, and re-layouts: 59.2 us -> 66.2 us
  starting transfers between devices: 0.08 us -> 6.49 us
    all_to_all x0 -> x1, waiting for transfers between devices: none -> 92.1 us  [body(): jax.lax.all_to_all(jnp.stack([references] * jax.lax.axis_size('img'), 0),...]
    all_gather x1 -> x0, waiting for transfers between devices: 81.7 us -> none  [body(): gathered = lax.all_gather(references, 'img', axis=0, tiled=True)]
    another operation x0 -> x2, local copies, waits for them, and re-layouts: none -> 10.2 us  [the longest x1 6.54 us: body(): gathered.reshape(IMAGE_SIDE, IMAGE_SIDE, -1)]
    all_to_all x0 -> x1, starting transfers between devices: none -> 6.49 us  [body(): jax.lax.all_to_all(jnp.stack([references] * jax.lax.axis_size('img'), 0),...]
    select_n x2, other arithmetic: 33.8 us -> 38.2 us  [select_turn(): jnp.where(rotations[None, None, :] == which, turner(field, which), result)]
  transfers between devices with their start and end apart: 2 -> 2, of which waited for: 2 -> 2; matrix products, arithmetic and copies ran while one was open for 1% -> 0% of each run, Pallas kernels for 0% -> 0%
where the time goes in v1:
time: 314 us; the launch traced here: 313 us
  waiting for transfers between devices  158 us (50%)
  local copies, waits for them, and re-layouts  66.2 us (21%)
  other arithmetic  44.2 us (14%)
  blocking collectives  15.7 us (5%)
  between operations  14.8 us (5%)
  matrix products  7.87 us (3%)
  starting transfers between devices  6.49 us (2%)
    all_to_all x1, waiting for transfers between devices, body(): jax.lax.all_to_all(jnp.stack([references] * jax.lax.axis_size('img'), 0),...  92.1 us
    reduce_scatter x1, waiting for transfers between devices, body(): owned = lax.psum_scatter(numerator, 'img', scatter_dimension=0, tiled=True)  65.7 us
    select_n x2, other arithmetic, select_turn(): jnp.where(rotations[None, None, :] == which, turner(field, which), result)  38.2 us
    rev x4, local copies, waits for them, and re-layouts, turn_forward(): return jnp.rot90(base, quarter, axes=(0, 1))  24.6 us
    rev x3, local copies, waits for them, and re-layouts, turn_inverse(): base = jnp.rot90(field, -quarter, axes=(0, 1))  18 us
    psum x1, blocking collectives, body(): weight_sum = lax.psum(jnp.sum(posterior, axis=0), 'img')  9.85 us
    reshape x1, local copies, waits for them, and re-layouts, body(): numer_image.reshape(IMAGE_SIDE, IMAGE_SIDE, -1)  6.57 us
    another operation x1, local copies, waits for them, and re-layouts, body(): gathered.reshape(IMAGE_SIDE, IMAGE_SIDE, -1)  6.54 us
  transfers between devices with their start and end apart: 2, of which 2 were waited for; matrix products, arithmetic and copies ran while one was open for 0% of the time, Pallas kernels for 0%

profile of v1, /device:TPU:0, one launch (start us, length us, event | category | flops | bytes accessed | tf_op | source)
XLA Modules:
  0.0 313.0 jit_solution(15143306080882097010)
XLA Ops:
  7.2 0.0 copy-start
  7.2 3.6 %stack.2 = f32[4,1024,256]{2,1,0:T(8,128)} broadcast(f32[1024,256]{1,0:T(8,128)} %param.8), dimensions={1,2} | broadcast | bytes 5242880 | tf_op jit(solution)/shard_map/stack | solution.py:49
  10.8 0.0 copy-start.6
  10.8 0.0 copy-start.4
  10.8 0.0 copy-start.5
  10.8 0.0 copy-start.3
  10.8 6.5 %all-to-all-start = ((f32[4,1024,256]{2,1,0:T(8,128)}), f32[4,1024,256]{2,1,0:T(8,128)}, u32[]{:S(2)}, u32[]{:S(2)}) async-start(f32[4,1024,256]{2,1,0:T(8,128)} %stack.2), calls=%async_computation | async-start | bytes 8388608 | tf_op jit(solution)/shard_map/all_to_all | solution.py:48
  17.3 0.0 reduce-scatter.2.cloned.1.call-start
  17.3 0.0 copy-done.6
  17.3 0.6 dynamic-slice
  18.6 0.0 copy-done.4
  18.6 0.0 copy-done.5
  18.6 0.1 select_reduce_fusion
  18.7 0.0 copy-done.3
  18.7 92.1 %all-to-all-done = f32[4,1024,256]{2,1,0:T(8,128)} async-done(((f32[4,1024,256]{2,1,0:T(8,128)}), f32[4,1024,256]{2,1,0:T(8,128)}, u32[]{:S(2)}, u32[]{:S(2)}) %all-to-all-start) | async-done | bytes 4194336 | tf_op jit(solution)/shard_map/all_to_all | solution.py:48
  110.8 6.7 %rev.40 = f32[64,64,256]{2,1,0:T(8,128)} reverse(f32[64,64,256]{2,1,0:T(8,128)} %bitcast.2), dimensions={1} | reverse | bytes 8388608 | tf_op jit(solution)/shard_map/jit(rot90)/jit(_flip)/rev | solution.py:29
  117.4 6.5 %copy.27 = f32[64,64,256]{2,0,1:T(8,128)} copy(f32[64,64,256]{2,1,0:T(8,128)} %bitcast.2) | data formatting | bytes 8388608 | tf_op jit(solution)/shard_map/reshape;reshape | solution.py:57
  124.0 2.7 multiply_reduce_fusion
  126.7 4.7 %rev.42 = f32[64,64,256]{2,0,1:T(8,128)} reverse(f32[64,64,256]{2,0,1:T(8,128)} %bitcast.4), dimensions={1} | reverse | bytes 8388608 | tf_op jit(solution)/shard_map/jit(rot90)/jit(_flip)/rev | solution.py:29
  131.4 6.6 %rev.41 = f32[64,64,256]{2,0,1:T(8,128)} reverse(f32[64,64,256]{2,0,1:T(8,128)} %copy.27), dimensions={0,1} | reverse | bytes 8388608 | tf_op jit(solution)/shard_map/jit(rot90)/jit(_flip)/rev | solution.py:29
  138.0 20.6 %fusion.9 = f32[64,64,256]{2,1,0:T(8,128)S(1)} fusion(f32[64,64,256]{2,1,0:T(8,128)} %rev.40, f32[64,64,256]{2,0,1:T(8,128)} %rev.42, f32[64,64,256]{2,0,1:T(8,128)} %rev.41, f32[64,64,256]{2,0,1:T(8,128)} %bitcast.4, f32[64,64,256]{2,0,1:T(8,128)} %bitcast.59, f32[64,64,256]{2,1,0:T(8,128)} %bitcast.2, pred[256]{0:T(512)(128)(4,1)S(1)} %get-tuple-element.162, ...), kind=kLoop, calls=%fused_computation.16 | loop fusion | flops 8388608 | bytes 29362176 | tf_op jit(solution)/shard_map/jit(_where)/select_n | solution.py:36
  158.6 0.0 copy-done
  158.7 2.6 fusion.14
  161.2 0.2 exponential_reduce_fusion
  161.4 0.2 dynamic-update-slice
  161.7 0.2 dynamic-update-slice.1
  161.9 5.8 %all-reduce.2 = (f32[384]{0:T(512)S(1)}, f32[384]{0:T(512)S(1)}) all-reduce(f32[384]{0:T(512)S(1)} %dynamic-update-slice, f32[384]{0:T(512)S(1)} %dynamic-update-slice.1), channel_id=2, replica_groups=mesh['groups'=2,'img'=4,'ref'=2,'rep'=2] {'ref','rep'}, use_global_device_ids=true, to_apply=%add | all-reduce | flops 768 | bytes 6144
  167.7 0.1 reshape.47
  167.8 0.1 reshape.48
  167.9 0.1 while.17
  168.0 0.0 copy-start.2
  168.0 5.3 %convolution_bitcast_fusion = f32[4096,256]{0,1:T(8,128)} fusion(f32[96,4096]{1,0:T(8,128)S(1)} %copy-done, f32[256,96]{0,1:T(8,128)S(1)} %get-tuple-element.165, f32[96]{0:T(128)S(1)} %log_add_fusion), kind=kOutput, calls=%fused_computation.6 | convolution fusion | flops 1207984128 | bytes 5865856 | tf_op jit(solution)/shard_map/dot_general | solution.py:74
  173.3 5.6 %copy.32 = f32[4096,256]{1,0:T(8,128)} copy(f32[4096,256]{0,1:T(8,128)} %convolution_bitcast_fusion) | data formatting | bytes 8388608 | tf_op jit(solution)/shard_map/dot_general | solution.py:74
  178.9 6.6 %copy.54 = f32[64,64,256]{2,0,1:T(8,128)} copy(f32[64,64,256]{2,1,0:T(8,128)} %bitcast.55) | data formatting | bytes 8388608 | tf_op jit(solution)/shard_map/reshape | solution.py:82
  185.5 6.7 %rev.45 = f32[64,64,256]{2,1,0:T(8,128)} reverse(f32[64,64,256]{2,1,0:T(8,128)} %bitcast.53), dimensions={1} | reverse | bytes 8388608 | tf_op jit(solution)/shard_map/jit(rot90)/jit(_flip)/rev | solution.py:24
  192.2 6.6 %rev.44 = f32[64,64,256]{2,1,0:T(8,128)} reverse(f32[64,64,256]{2,1,0:T(8,128)} %bitcast.54), dimensions={0,1} | reverse | bytes 8388608 | tf_op jit(solution)/shard_map/jit(rot90)/jit(_flip)/rev | solution.py:24
  198.8 4.7 %rev.43 = f32[64,64,256]{2,0,1:T(8,128)} reverse(f32[64,64,256]{2,0,1:T(8,128)} %copy.54), dimensions={1} | reverse | bytes 8388608 | tf_op jit(solution)/shard_map/jit(rot90)/jit(_flip)/rev | solution.py:24
  203.5 6.6 %rev.46 = f32[64,64,256]{2,1,0:T(8,128)} reverse(f32[64,64,256]{2,1,0:T(8,128)} %bitcast.56), dimensions={0,1} | reverse | bytes 8388608 | tf_op jit(solution)/shard_map/jit(rot90)/jit(_flip)/rev | solution.py:24
  210.1 0.0 copy-start.1
  210.1 17.5 %fusion.7 = f32[64,64,256]{2,1,0:T(8,128)} fusion(f32[64,64,256]{2,1,0:T(8,128)} %rev.44, f32[64,64,256]{2,1,0:T(8,128)} %rev.45, f32[64,64,256]{2,1,0:T(8,128)} %rev.46, f32[64,64,256]{2,0,1:T(8,128)} %rev.43, f32[64,64,256]{2,0,1:T(8,128)} %bitcast.58, f32[64,64,256]{2,1,0:T(8,128)} %bitcast.57, pred[256]{0:T(512)(128)(4,1)S(1)} %get-tuple-element.162, ...), kind=kLoop, calls=%fused_computation.13 | loop fusion | flops 8388608 | bytes 29362176 | tf_op jit(solution)/shard_map/jit(_where)/select_n | solution.py:36
  227.6 0.0 reduce-scatter.2.cloned.1.call-update
  227.7 0.0 copy-done.2
  227.7 0.1 fusion.11
  227.8 9.8 %psum.7 = f32[256]{0:T(256)S(1)} all-reduce(f32[256]{0:T(256)S(1)} %fusion.11), channel_id=1, replica_groups=mesh['groups'=2,'img'=4,'ref'=2,'rep'=2] {'img'}, use_global_device_ids=true, to_apply=%region_8.9 | all-reduce | flops 256 | bytes 2048 | tf_op jit(solution)/shard_map/psum | solution.py:73
  237.6 0.6 broadcast_multiply_fusion
  238.2 65.7 %reduce-scatter.2.cloned.1.call-done = f32[1024,256]{1,0:T(8,128)} async-done(((f32[4096,256]{1,0:T(8,128)}), f32[1024,256]{1,0:T(8,128)}) %reduce-scatter.2.cloned.1.call-update) | async-done | bytes 1048592 | tf_op jit(solution)/shard_map/reduce_scatter | solution.py:84
  303.9 2.3 broadcast_divide_fusion
  306.2 0.0 copy-done.1
  (10 shorter events, 0.1 us)
Async XLA Ops:
  7.2 151.5 %copy-start = (f32[96,4096]{1,0:T(8,128)S(1)}, f32[96,4096]{1,0:T(8,128)}, u32[]{:S(2)}) copy-start(f32[96,4096]{1,0:T(8,128)} %param.7) | copy-start | bytes 4718596
  10.8 6.5 %copy-start.6 = (u32[32]{0:T(128)S(1)}, u32[32]{0:T(128)}, u32[]{:S(2)}) copy-start(u32[32]{0:T(128)} %constant.75) | copy-start | bytes 388
  10.8 7.7 %copy-start.4 = (f32[16]{0:T(128)S(1)}, f32[16]{0:T(128)}, u32[]{:S(2)}) copy-start(f32[16]{0:T(128)} %param.11) | copy-start | bytes 196
  10.8 7.7 %copy-start.5 = (s32[96]{0:T(128)S(1)}, s32[96]{0:T(128)}, u32[]{:S(2)}) copy-start(s32[96]{0:T(128)} %param.10) | copy-start | bytes 1156
  10.8 7.8 %copy-start.3 = (s32[256]{0:T(256)S(1)}, s32[256]{0:T(256)}, u32[]{:S(2)}) copy-start(s32[256]{0:T(256)} %param.9) | copy-start | bytes 3076
  10.8 99.9 %all-to-all-start = ((f32[4,1024,256]{2,1,0:T(8,128)}), f32[4,1024,256]{2,1,0:T(8,128)}, u32[]{:S(2)}, u32[]{:S(2)}) async-start(f32[4,1024,256]{2,1,0:T(8,128)} %stack.2), calls=%async_computation | async-start | bytes 8388608 | tf_op jit(solution)/shard_map/all_to_all | solution.py:48
  17.3 286.6 %reduce-scatter.2.cloned.1.call-start = ((), (), s32[]{:S(2)}) async-start(), calls=%async_computation.2 | async-start | bytes 5242880 | tf_op jit(solution)/shard_map/reduce_scatter | solution.py:84
  168.0 59.7 %copy-start.2 = (f32[96]{0:T(128)}, f32[96]{0:T(128)S(1)}, u32[]{:S(2)}) copy-start(f32[96]{0:T(128)S(1)} %log_add_fusion) | copy-start | bytes 1156
  210.1 96.1 %copy-start.1 = (f32[96,4096]{1,0:T(8,128)S(1)}, f32[96,4096]{1,0:T(8,128)}, u32[]{:S(2)}) copy-start(f32[96,4096]{1,0:T(8,128)} %param.7) | copy-start | bytes 4718596
Sparse Core Ops, SparseCore 0:
  227.8 76.0 reduce-scatter.1
